TPU v7x, 128 devices: a whole 4x4x4 slice. The times are simulated.
128 devices in a mesh: expert: 4 (over z), panel: 32 (over y, x, core).
Axes of the slice: x: 4, y: 4, z: 4, core: 2. Of those that a mesh axis runs over, the one named last changes fastest.
Arguments:
- tokens: bfloat16 [4096, 6144], P(('expert', 'panel')), may hold values from -6 to 6
- routes: int32 [4096, 2], P(('expert', 'panel')), may hold values from 0 to 7, all different within a row; in each aligned block of 32 rows (0 to 31, 32 to 63, ...) at most 12 rows name the same one
- router_weights: float32 [4096, 2], P(('expert', 'panel')), may hold values from 0.05 to 0.95
Outputs:
- hessian: float32 [8, 6144, 6144], P('expert', 'panel')
Inputs may be any that keep to these rules, and one draw needn't show every extreme that they name: `routes`: each row names two different experts; among the 32 rows of one device no expert is named more than 12 times, a bound that some block reaches.
All inputs are finite; a program needn't handle non-finite values.
Results may differ from a plain program's by a relative error of at most 0.0036.
Values may be sent and summed in bfloat16 or wider, within the bound.
A program may use at most 192 MiB of HBM per device.

v0:
```python
import jax
import jax.numpy as jnp
from jax import lax
from jax.sharding import PartitionSpec as P

EXPERTS = 8
CAP = 12


def per_device(tokens, routes, router_weights):
    count, width = tokens.shape
    groups = lax.axis_size("expert")
    panels = lax.axis_size("panel")
    quarter = width // groups
    panel_width = width // panels
    scaling = float(groups * panels * CAP) ** (-0.5)
    rounded = router_weights.astype(jnp.bfloat16)
    ids = jnp.arange(64, dtype=jnp.int32)[None, :]
    zero = jnp.zeros((), jnp.bfloat16)
    dense = jnp.where(routes[:, 0:1] == ids, rounded[:, 0:1], zero) + jnp.where(
        routes[:, 1:2] == ids, rounded[:, 1:2], zero
    )
    seed = lax.all_to_all(
        tokens.reshape(count, groups, quarter), "expert", split_axis=1, concat_axis=0, tiled=True
    ).reshape(groups * count, quarter)
    columns = lax.all_gather(seed, "panel", axis=0, tiled=True)
    rows = jnp.concatenate(
        [
            tokens.reshape(count, panels, panel_width),
            jnp.broadcast_to(dense[:, None, :], (count, panels, 64)),
        ],
        axis=2,
    )
    rows = lax.all_to_all(rows, "panel", split_axis=1, concat_axis=0, tiled=True)
    rows = rows.reshape(panels * count, panel_width + 64)
    rows = lax.all_gather(rows, "expert", axis=0, tiled=True)
    rows = rows.reshape(groups, panels, count, panel_width + 64).transpose(3, 1, 0, 2)
    rows = rows.reshape(panel_width + 64, -1)
    weights = rows[panel_width : panel_width + EXPERTS]
    scaled = (weights[:, None, :] * rows[None, :panel_width, :]).reshape(-1, rows.shape[1])
    blocks = jnp.dot(scaled, columns, preferred_element_type=jnp.float32) * scaling
    blocks = blocks.astype(jnp.bfloat16).reshape(groups, EXPERTS // groups, panel_width, quarter)
    blocks = lax.all_to_all(blocks, "expert", split_axis=0, concat_axis=0, tiled=True)
    return blocks.transpose(1, 2, 0, 3).reshape(-1, panel_width, width).astype(jnp.float32)


def solution(mesh):
    placed = (
        P(("expert", "panel"), None),
        P(("expert", "panel"), None),
        P(("expert", "panel"), None),
    )
    return jax.shard_map(
        per_device,
        mesh=mesh,
        in_specs=placed,
        out_specs=P("expert", "panel", None),
        check_vma=False,
    )
```

profile of v0, /device:TPU:1, one launch (start us, length us, event | category | flops | bytes accessed | tf_op | source)
XLA Modules:
  0.0 222.1 jit_solution(15191602077753477741)
XLA Ops:
  6.5 0.0 all-gather.3.cloned.1.call-start
  6.5 0.7 convert_element_type.15
  7.2 0.8 slice_bitcast_fusion.3
  8.0 1.6 reshape.97
  9.6 0.1 fusion.3
  9.8 0.2 pad_maximum_fusion
  9.9 0.3 copy.15
  10.2 20.0 %all_to_all.35 = bf16[32,32,256]{2,0,1:T(8,128)(2,1)} all-to-all(bf16[32,32,256]{2,0,1:T(8,128)(2,1)S(1)} %copy.15), channel_id=1, replica_groups=mesh['expert'=4,'panel'=32] {'panel'}, dimensions={1} | all-to-all | bytes 1048576 | tf_op jit(solution)/shard_map/all_to_all | solution.py:34
  30.3 0.0 all-gather.3.cloned.1.call-update
  30.3 0.0 all-gather.5.cloned.1.call-start
  30.3 1.0 copy.27
  31.4 12.3 %all_to_all.36 = bf16[32,4,1536]{2,0,1:T(8,128)(2,1)} all-to-all(bf16[32,4,1536]{2,0,1:T(8,128)(2,1)S(1)} %bitcast.46), channel_id=1, replica_groups=mesh['expert'=4,'panel'=32] {'expert'}, dimensions={1} | all-to-all | bytes 786432 | tf_op jit(solution)/shard_map/all_to_all | solution.py:23
  43.7 0.0 all-gather.5.cloned.1.call-update
  43.7 18.0 %all-gather.3.cloned.1.call-done = bf16[4096,256]{1,0:T(8,128)(2,1)} async-done(((bf16[1024,256]{1,0:T(8,128)(2,1)}), bf16[4096,256]{1,0:T(8,128)(2,1)}) %all-gather.3.cloned.1.call-update) | async-done | bytes 2097168 | tf_op jit(solution)/shard_map/all_gather | solution.py:36
  61.7 1.8 copy.26
  63.6 0.4 slice.26
  64.0 0.3 copy.21
  64.3 2.7 %copy.18 = bf16[192,4096]{1,0:T(8,128)(2,1)} copy(bf16[192,4096]{0,1:T(8,128)(2,1)S(1)} %bitcast.38) | data formatting | bytes 3145728 | tf_op jit(solution)/shard_map/mul | solution.py:40
  67.0 6.8 %broadcast_multiply_fusion = bf16[8,192,4096]{2,1,0:T(8,128)(2,1)} fusion(bf16[192,4096]{1,0:T(8,128)(2,1)} %copy.18, bf16[8,4096]{1,0:T(8,128)(2,1)S(1)} %copy.21), kind=kLoop, calls=%fused_computation.3 | loop fusion | flops 6291456 | bytes 14221312 | tf_op jit(solution)/shard_map/mul | solution.py:40
  73.8 51.5 %all-gather.5.cloned.1.call-done = bf16[4096,1536]{1,0:T(8,128)(2,1)} async-done(((bf16[128,1536]{1,0:T(8,128)(2,1)}), bf16[4096,1536]{1,0:T(8,128)(2,1)}) %all-gather.5.cloned.1.call-update) | async-done | bytes 12582928 | tf_op jit(solution)/shard_map/all_gather | solution.py:26
  125.3 26.0 %fusion = bf16[1536,1536]{1,0:T(8,128)(2,1)S(1)} fusion(bf16[1536,4096]{1,0:T(8,128)(2,1)} %bitcast.39, bf16[4096,1536]{1,0:T(8,128)(2,1)} %all-gather.5.cloned.1.call-done), kind=kOutput, calls=%fused_computation.2 | convolution fusion | flops 19332071424 | bytes 29884416 | tf_op jit(solution)/shard_map/dot_general | solution.py:41
  151.4 57.9 %all_to_all.37 = bf16[4,2,192,1536]{3,2,1,0:T(8,128)(2,1)S(1)} all-to-all(bf16[4,2,192,1536]{3,2,1,0:T(8,128)(2,1)S(1)} %bitcast.40), channel_id=1, replica_groups=mesh['expert'=4,'panel'=32] {'expert'}, dimensions={0} | all-to-all | bytes 9437184 | tf_op jit(solution)/shard_map/all_to_all | solution.py:43
  209.3 1.3 convert_bitcast_fusion
  210.6 4.6 %copy.23 = f32[4,2,24,8,1536]{4,3,0,2,1:T(8,128)} copy(f32[4,2,24,8,1536]{4,3,2,1,0:T(8,128)S(1)} %convert_bitcast_fusion) | data formatting | bytes 18874368 | tf_op jit(solution)/shard_map/convert_element_type | solution.py:44
  (2 shorter events, 0.0 us)
Async XLA Ops:
  6.5 55.2 %all-gather.3.cloned.1.call-start = ((), (), s32[]{:S(2)}) async-start(), calls=%async_computation.3 | async-start | bytes 2621440 | tf_op jit(solution)/shard_map/all_gather | solution.py:36
  30.3 95.0 %all-gather.5.cloned.1.call-start = ((), (), s32[]{:S(2)}) async-start(), calls=%async_computation.4 | async-start | bytes 12976128 | tf_op jit(solution)/shard_map/all_gather | solution.py:26
Sparse Core Ops, SparseCore 0:
  30.4 31.2 all-gather.2
  64.0 61.3 all-gather.4
where the time goes:
time: 222 us
  blocking collectives  90.3 us (41%)
  waiting for transfers between devices  69.6 us (31%)
  matrix products  26 us (12%)
  local copies, waits for them, and re-layouts  13.6 us (6%)
  between operations  13.5 us (6%)
  other arithmetic  9.06 us (4%)
    all_to_all x1, blocking collectives, per_device(): lax.all_to_all(blocks, 'expert', split_axis=0, concat_axis=0, tiled=True)  57.9 us
    all_gather x1, waiting for transfers between devices, per_device(): columns = lax.all_gather(seed, 'panel', axis=0, tiled=True)  51.5 us
    dot_general x1, matrix products, per_device(): jnp.dot(scaled, columns, preferred_element_type=jnp.float32) * scaling  26 us
    all_to_all x1, blocking collectives, per_device(): lax.all_to_all(rows, 'panel', split_axis=1, concat_axis=0, tiled=True)  20 us
    all_gather x1, waiting for transfers between devices, per_device(): rows = lax.all_gather(rows, 'expert', axis=0, tiled=True)  18 us
    all_to_all x1, blocking collectives, per_device(): lax.all_to_all(tokens.reshape(count, groups, quarter), 'expert', split_ax...  12.3 us
    mul x1, other arithmetic, per_device(): weights[:, None, :] * rows[None, :panel_width, :]  6.83 us
    convert_element_type x1, local copies, waits for them, and re-layouts, per_device(): blocks.transpose(1, 2, 0, 3).reshape(-1, panel_width, width)  4.6 us
  transfers between devices with their start and end apart: 2, of which 2 were waited for; matrix products, arithmetic and copies ran while one was open for 6% of the time, Pallas kernels for 0%

commit v1 on v0

--- a/solution.py
+++ b/solution.py
@@ -33,7 +33,14 @@
     )
     rows = lax.all_to_all(rows, "panel", split_axis=1, concat_axis=0, tiled=True)
     rows = rows.reshape(panels * count, panel_width + 64)
-    rows = lax.all_gather(rows, "expert", axis=0, tiled=True)
+    ring = [rows]
+    for hop in range(3):
+        ring.append(lax.ppermute(ring[-1], "expert", [(dev, (dev + 1) % 4) for dev in range(4)]))
+    rows = jnp.roll(
+        jnp.concatenate(ring[::-1], axis=0),
+        (lax.axis_index("expert") + 1) * ring[0].shape[0],
+        axis=0,
+    )
     rows = rows.reshape(groups, panels, count, panel_width + 64).transpose(3, 1, 0, 2)
     rows = rows.reshape(panel_width + 64, -1)
     weights = rows[panel_width : panel_width + EXPERTS]

time: 222 us -> 198 us (0.89)
  the two profiles are of different devices: /device:TPU:1 before, /device:TPU:8 now
where the time goes in v1:
time: 198 us
  blocking collectives  89.9 us (45%)
  waiting for transfers between devices  45.3 us (23%)
  matrix products  26 us (13%)
  local copies, waits for them, and re-layouts  14.5 us (7%)
  between operations  13.5 us (7%)
  other arithmetic  7.57 us (4%)
    all_to_all x1, blocking collectives, per_device(): lax.all_to_all(blocks, 'expert', split_axis=0, concat_axis=0, tiled=True)  56.5 us
    ppermute x3, waiting for transfers between devices, per_device(): lax.ppermute(ring[-1], 'expert', [(dev, (dev + 1) % 4) for dev in range(4)])  45.3 us
    dot_general x1, matrix products, per_device(): jnp.dot(scaled, columns, preferred_element_type=jnp.float32) * scaling  26 us
    all_to_all x1, blocking collectives, per_device(): lax.all_to_all(rows, 'panel', split_axis=1, concat_axis=0, tiled=True)  20.1 us
    all_to_all x1, blocking collectives, per_device(): lax.all_to_all(tokens.reshape(count, groups, quarter), 'expert', split_ax...  13.3 us
    mul x1, other arithmetic, per_device(): weights[:, None, :] * rows[None, :panel_width, :]  5.34 us
    convert_element_type x1, local copies, waits for them, and re-layouts, per_device(): blocks.transpose(1, 2, 0, 3).reshape(-1, panel_width, width)  4.6 us
  transfers between devices with their start and end apart: 4, of which 3 were waited for; matrix products, arithmetic and copies ran while one was open for 8% of the time, Pallas kernels for 0%

profile of v1, /device:TPU:8, one launch (start us, length us, event | category | flops | bytes accessed | tf_op | source)
XLA Modules:
  0.0 197.8 jit_solution(9773385992295185005)
XLA Ops:
  6.5 0.0 all-gather.2.cloned.1.call-start
  6.5 1.0 copy.23
  7.6 13.3 %all_to_all.35 = bf16[32,4,1536]{2,0,1:T(8,128)(2,1)} all-to-all(bf16[32,4,1536]{2,0,1:T(8,128)(2,1)S(1)} %bitcast.45), channel_id=1, replica_groups=mesh['expert'=4,'panel'=32] {'expert'}, dimensions={1} | all-to-all | bytes 786432 | tf_op jit(solution)/shard_map/all_to_all | solution.py:23
  20.8 0.0 all-gather.2.cloned.1.call-update
  20.9 1.6 reshape.97
  22.5 0.7 convert_element_type.15
  23.2 0.8 slice_bitcast_fusion.3
  24.0 0.1 fusion.3
  24.1 0.2 pad_maximum_fusion
  24.3 0.3 copy.14
  24.6 20.1 %all_to_all.36 = bf16[32,32,256]{2,0,1:T(8,128)(2,1)S(1)} all-to-all(bf16[32,32,256]{2,0,1:T(8,128)(2,1)S(1)} %copy.14), channel_id=1, replica_groups=mesh['expert'=4,'panel'=32] {'panel'}, dimensions={1} | all-to-all | bytes 1048576 | tf_op jit(solution)/shard_map/all_to_all | solution.py:34
  44.6 0.8 collective-permute-start
  45.5 14.7 %collective-permute-done = bf16[1024,256]{1,0:T(8,128)(2,1)S(1)} collective-permute-done((bf16[1024,256]{1,0:T(8,128)(2,1)S(1)}, bf16[1024,256]{1,0:T(8,128)(2,1)S(1)}, u32[]{:S(2)}, u32[]{:S(2)}) %collective-permute-start) | collective-permute-done | bytes 524320 | tf_op jit(solution)/shard_map/ppermute | solution.py:38
  60.2 0.1 collective-permute-start.1
  60.3 15.6 %collective-permute-done.1 = bf16[1024,256]{1,0:T(8,128)(2,1)S(1)} collective-permute-done((bf16[1024,256]{1,0:T(8,128)(2,1)S(1)}, bf16[1024,256]{1,0:T(8,128)(2,1)S(1)}, u32[]{:S(2)}, u32[]{:S(2)}) %collective-permute-start.1) | collective-permute-done | bytes 524320 | tf_op jit(solution)/shard_map/ppermute | solution.py:38
  75.9 0.0 collective-permute-start.2
  75.9 15.0 %collective-permute-done.2 = bf16[1024,256]{1,0:T(8,128)(2,1)S(1)} collective-permute-done((bf16[1024,256]{1,0:T(8,128)(2,1)S(1)}, bf16[1024,256]{1,0:T(8,128)(2,1)S(1)}, u32[]{:S(2)}, u32[]{:S(2)}) %collective-permute-start.2) | collective-permute-done | bytes 524320 | tf_op jit(solution)/shard_map/ppermute | solution.py:38
  91.3 0.1 constant_dynamic-slice_fusion
  91.4 0.4 slice.26
  91.8 0.6 copy.15
  92.4 0.3 mul.31
  92.7 1.6 copy.16
  94.3 2.9 %copy.17 = bf16[192,4096]{1,0:T(8,128)(2,1)S(1)} copy(bf16[192,4096]{0,1:T(8,128)(2,1)} %bitcast.38) | data formatting | bytes 3145728 | tf_op jit(solution)/shard_map/mul | solution.py:47
  97.1 5.3 %broadcast_multiply_fusion = bf16[8,192,4096]{2,1,0:T(8,128)(2,1)} fusion(bf16[192,4096]{1,0:T(8,128)(2,1)S(1)} %copy.17, bf16[8,4096]{1,0:T(8,128)(2,1)S(1)} %mul.31), kind=kLoop, calls=%fused_computation.3 | loop fusion | flops 6291456 | bytes 14221312 | tf_op jit(solution)/shard_map/mul | solution.py:47
  102.5 0.0 all-gather.2.cloned.1.call-done
  102.5 26.0 %fusion = bf16[1536,1536]{1,0:T(8,128)(2,1)S(1)} fusion(bf16[1536,4096]{1,0:T(8,128)(2,1)} %bitcast.37, bf16[4096,1536]{1,0:T(8,128)(2,1)} %all-gather.2.cloned.1.call-done), kind=kOutput, calls=%fused_computation.2 | convolution fusion | flops 19332071424 | bytes 29884416 | tf_op jit(solution)/shard_map/dot_general | solution.py:48
  128.5 56.5 %all_to_all.37 = bf16[4,2,192,1536]{3,2,1,0:T(8,128)(2,1)S(1)} all-to-all(bf16[4,2,192,1536]{3,2,1,0:T(8,128)(2,1)S(1)} %bitcast.39), channel_id=1, replica_groups=mesh['expert'=4,'panel'=32] {'expert'}, dimensions={0} | all-to-all | bytes 9437184 | tf_op jit(solution)/shard_map/all_to_all | solution.py:50
  185.1 1.3 convert_bitcast_fusion
  186.4 4.6 %copy.21 = f32[4,2,24,8,1536]{4,3,0,2,1:T(8,128)} copy(f32[4,2,24,8,1536]{4,3,2,1,0:T(8,128)S(1)} %convert_bitcast_fusion) | data formatting | bytes 18874368 | tf_op jit(solution)/shard_map/convert_element_type | solution.py:51
  (10 shorter events, 0.3 us)
Async XLA Ops:
  6.5 95.9 %all-gather.2.cloned.1.call-start = ((), (), s32[]{:S(2)}) async-start(), calls=%async_computation.3 | async-start | bytes 12976128 | tf_op jit(solution)/shard_map/all_gather | solution.py:26
  44.6 15.5 %collective-permute-start = (bf16[1024,256]{1,0:T(8,128)(2,1)S(1)}, bf16[1024,256]{1,0:T(8,128)(2,1)S(1)}, u32[]{:S(2)}, u32[]{:S(2)}) collective-permute-start(bf16[1024,256]{1,0:T(8,128)(2,1)S(1)} %bitcast.40), channel_id=1, source_target_pairs={{0,32},{32,64},{64,96},{96,0},{1,33},{33,65},{65,97},{97,1},{2,34}... | collective-permute-start | bytes 1572872 | tf_op jit(solution)/shard_map/ppermute | solution.py:38
  60.2 15.7 %collective-permute-start.1 = (bf16[1024,256]{1,0:T(8,128)(2,1)S(1)}, bf16[1024,256]{1,0:T(8,128)(2,1)S(1)}, u32[]{:S(2)}, u32[]{:S(2)}) collective-permute-start(bf16[1024,256]{1,0:T(8,128)(2,1)S(1)} %collective-permute-done), channel_id=1, source_target_pairs={{0,32},{32,64},{64,96},{96,0},{1,33},{33,65},{65,97},{97,1},{2,34}... | collective-permute-start | bytes 1572872 | tf_op jit(solution)/shard_map/ppermute | solution.py:38
  75.9 15.0 %collective-permute-start.2 = (bf16[1024,256]{1,0:T(8,128)(2,1)S(1)}, bf16[1024,256]{1,0:T(8,128)(2,1)S(1)}, u32[]{:S(2)}, u32[]{:S(2)}) collective-permute-start(bf16[1024,256]{1,0:T(8,128)(2,1)S(1)} %collective-permute-done.1), channel_id=1, source_target_pairs={{0,32},{32,64},{64,96},{96,0},{1,33},{33,65},{65,97},{97,1},{2,34}... | collective-permute-start | bytes 1572872 | tf_op jit(solution)/shard_map/ppermute | solution.py:38
Sparse Core Ops, SparseCore 0:
  21.0 65.1 all-gather.1
